TPU v7x, 32 devices: a whole 2x2x4 slice. The times are simulated.
32 devices in a mesh: rep: 8 (over y, x, core), fsdp: 4 (over z).
Axes of the slice: x: 2, y: 2, z: 4, core: 2. Of those that a mesh axis runs over, the one named last changes fastest.
Arguments:
- base: float32 [3, 32, 8192], P(None, 'fsdp'), may hold values from -6 to 6
- local: float32 [8, 3, 32, 8192], P('rep', None, 'fsdp'), may hold values from -6 to 6
- momentum: float32 [3, 32, 8192], P(None, 'fsdp', 'rep'), may hold values from -3 to 3
- hidden: bfloat16 [8, 512, 32], P('rep', 'fsdp'), may hold values from -6 to 6
- out_grad: bfloat16 [8, 512, 8192], P('rep', 'fsdp'), may hold values from -0.06591797 to 0.06591797
Outputs:
- mixed: float32 [8, 3, 32, 8192], P('rep', None, 'fsdp')
- momentum_out: float32 [3, 32, 8192], P(None, 'fsdp', 'rep')
- input_grad: bfloat16 [8, 512, 32], P('rep', 'fsdp')
- weight_grad: float32 [8, 32, 8192], P('rep', 'fsdp')
All inputs are finite; a program needn't handle non-finite values.
Results may differ from a plain program's by a relative error of at most 0.015.
Values may be sent and summed in bfloat16 or wider, within the bound.
No kernel may reach another device: no remote copies, remote signals or barrier semaphores. Data moves between devices by JAX's collectives and lax.ppermute only.
A program may use at most 64 MiB of HBM per device.

v0:
```python
import jax
import jax.numpy as jnp
from jax import lax
from jax.sharding import PartitionSpec as P

outer_beta = 0.9
outer_rate = 0.7
mix_keep = 0.5


def per_device(base, local, momentum, hidden, out_grad):
    replica_count = lax.axis_size("rep")
    weights = local[0, 2].astype(jnp.bfloat16)
    grads_here = out_grad[0]
    activations = hidden[0]
    input_grad = lax.dot_general(
        grads_here,
        lax.all_gather(weights, "fsdp", axis=0, tiled=True),
        (((1,), (1,)), ((), ())),
        preferred_element_type=jnp.float32,
    ).astype(jnp.bfloat16)
    weight_grad = lax.psum_scatter(
        lax.dot_general(
            activations, grads_here, (((0,), (0,)), ((), ())), preferred_element_type=jnp.float32
        ).astype(jnp.bfloat16),
        "fsdp",
        scatter_dimension=0,
        tiled=True,
    ).astype(jnp.float32)
    drift = base - local[0]
    share_width = momentum.shape[2]
    share_start = lax.axis_index("rep") * share_width
    delta = lax.psum(drift, "rep") / replica_count
    moment_all = lax.all_gather(momentum, "rep", axis=2, tiled=True)
    moment_new = outer_beta * moment_all + delta
    updated = base - outer_rate * (delta + outer_beta * moment_new)
    momentum_out = lax.dynamic_slice_in_dim(moment_new, share_start, share_width, 2)
    mixed = mix_keep * local[0] + (1.0 - mix_keep) * updated
    return (mixed[None], momentum_out, input_grad[None], weight_grad[None])


def solution(mesh):
    return jax.shard_map(
        per_device,
        mesh=mesh,
        in_specs=(
            P(None, "fsdp", None),
            P("rep", None, "fsdp", None),
            P(None, "fsdp", "rep"),
            P("rep", "fsdp", None),
            P("rep", "fsdp", None),
        ),
        out_specs=(
            P("rep", None, "fsdp", None),
            P(None, "fsdp", "rep"),
            P("rep", "fsdp", None),
            P("rep", "fsdp", None),
        ),
        check_vma=False,
    )
```

profile of v0, /device:TPU:0, one launch (start us, length us, event | category | flops | bytes accessed | tf_op | source)
XLA Modules:
  0.0 83.5 jit_solution(2399152442900048808)
XLA Ops:
  8.0 0.0 copy-start
  8.0 0.0 copy-start.3
  8.0 0.0 all-reduce.2.cloned.1.call-start
  8.1 2.5 %bitcast_subtract_fusion = f32[3,8,8192]{2,1,0:T(8,128)} fusion(f32[3,8,8192]{2,1,0:T(8,128)} %param.5, f32[1,3,8,8192]{3,2,1,0:T(8,128)} %param.6), kind=kLoop, calls=%fused_computation.7 | loop fusion | flops 196608 | bytes 2359296 | tf_op jit(solution)/shard_map/sub | solution.py:30
  10.5 0.0 copy-start.1
  10.5 0.0 copy-start.2
  10.5 0.0 all-reduce.2.cloned.1.call-update
  10.6 0.0 reduce-scatter.2.cloned.1.call-start
  10.6 0.0 copy-done
  10.6 0.0 copy-done.3
  10.6 1.2 %convolution_convert_fusion = bf16[32,8192]{1,0:T(8,128)(2,1)} fusion(bf16[1,128,8192]{2,1,0:T(8,128)(2,1)S(1)} %copy-done, bf16[1,128,32]{1,2,0:T(8,128)(2,1)S(1)} %copy-done.3), kind=kOutput, calls=%fused_computation | convolution fusion | flops 67371008 | bytes 2629632 | tf_op jit(solution)/shard_map/dot_general | solution.py:23
  11.8 0.0 reduce-scatter.2.cloned.1.call-update
  11.9 0.0 copy-done.1
  11.9 0.0 copy-done.2
  11.9 14.0 %all_gather.6 = f32[3,8,8192]{2,1,0:T(8,128)} all-gather(f32[3,8,1024]{2,1,0:T(8,128)S(1)} %copy-done.2), channel_id=1, replica_groups=mesh['rep'=8,'fsdp'=4] {'rep'}, dimensions={2}, use_global_device_ids=true | all-gather | bytes 884736 | tf_op jit(solution)/shard_map/all_gather | solution.py:34
  25.9 18.9 %all-gather = bf16[1,1,32,8192]{3,2,1,0:T(8,128)(2,1)S(1)} all-gather(bf16[1,1,8,8192]{3,2,1,0:T(8,128)(2,1)S(1)} %slice.7), channel_id=2, replica_groups=mesh['rep'=8,'fsdp'=4] {'fsdp'}, dimensions={2}, use_global_device_ids=true | all-gather | bytes 655360 | tf_op jit(solution)/shard_map/all_gather | solution.py:18
  44.8 1.4 %fusion.6 = bf16[1,128,32]{1,2,0:T(8,128)(2,1)} fusion(bf16[1,128,8192]{2,1,0:T(8,128)(2,1)S(1)} %copy-done, bf16[1,1,32,8192]{3,2,1,0:T(8,128)(2,1)S(1)} %all-gather), kind=kOutput, calls=%fused_computation.5 | convolution fusion | flops 67112960 | bytes 2629632 | tf_op jit(solution)/shard_map/dot_general | solution.py:16
  46.2 24.9 %all-reduce.2.cloned.1.call-done = f32[3,8,8192]{2,1,0:T(8,128)} async-done(((f32[3,8,8192]{2,1,0:T(8,128)}), f32[3,8,8192]{2,1,0:T(8,128)}) %all-reduce.2.cloned.1.call-update) | async-done | bytes 786448 | tf_op jit(solution)/shard_map/psum | solution.py:33
  71.1 2.7 %multiply_add_fusion = (f32[3,8,8192]{2,1,0:T(8,128)S(1)}, f32[1,3,8,8192]{3,2,1,0:T(8,128)}) fusion(f32[3,8,8192]{2,1,0:T(8,128)} %all_gather.6, f32[3,8,8192]{2,1,0:T(8,128)} %all-reduce.2.cloned.1.call-done, f32[3,8,8192]{2,1,0:T(8,128)} %param.5, f32[1,3,8,8192]{3,2,1,0:T(8,128)S(1)} %copy-done.1), kind=kLoop, calls=%fused_computation.10 | loop fusion | flops 1769472 | bytes 4718592 | tf_op jit(solution)/shard_map/add | solution.py:35
  73.8 0.6 constant_dynamic-slice_fusion
  74.5 0.0 reduce-scatter.2.cloned.1.call-done
  74.5 1.6 %bitcast_convert_fusion = f32[1,8,8192]{2,1,0:T(8,128)} fusion(bf16[8,8192]{1,0:T(8,128)(2,1)} %reduce-scatter.2.cloned.1.call-done), kind=kLoop, calls=%fused_computation.13 | loop fusion | flops 65536 | bytes 393216 | tf_op jit(solution)/shard_map/broadcast_in_dim | solution.py:39
  (1 shorter events, 0.0 us)
Async XLA Ops:
  8.0 2.6 %copy-start = (bf16[1,128,8192]{2,1,0:T(8,128)(2,1)S(1)}, bf16[1,128,8192]{2,1,0:T(8,128)(2,1)}, u32[]{:S(2)}) copy-start(bf16[1,128,8192]{2,1,0:T(8,128)(2,1)} %param.9) | copy-start | bytes 6291460
  8.0 2.6 %copy-start.3 = (bf16[1,128,32]{1,2,0:T(8,128)(2,1)S(1)}, bf16[1,128,32]{1,2,0:T(8,128)(2,1)}, u32[]{:S(2)}) copy-start(bf16[1,128,32]{1,2,0:T(8,128)(2,1)} %param.8) | copy-start | bytes 24580
  8.0 63.1 %all-reduce.2.cloned.1.call-start = ((), (), s32[]{:S(2)}) async-start(), calls=%async_computation.1 | async-start | bytes 1572864 | tf_op jit(solution)/shard_map/psum | solution.py:33
  10.5 1.3 %copy-start.1 = (f32[1,3,8,8192]{3,2,1,0:T(8,128)S(1)}, f32[1,3,8,8192]{3,2,1,0:T(8,128)}, u32[]{:S(2)}) copy-start(f32[1,3,8,8192]{3,2,1,0:T(8,128)} %param.6) | copy-start | bytes 2359300
  10.5 1.4 %copy-start.2 = (f32[3,8,1024]{2,1,0:T(8,128)S(1)}, f32[3,8,1024]{2,1,0:T(8,128)}, u32[]{:S(2)}) copy-start(f32[3,8,1024]{2,1,0:T(8,128)} %param.7) | copy-start | bytes 294916
  10.6 63.9 %reduce-scatter.2.cloned.1.call-start = ((), (), s32[]{:S(2)}) async-start(), calls=%async_computation.2 | async-start | bytes 655360 | tf_op jit(solution)/shard_map/reduce_scatter | solution.py:22
Sparse Core Ops, SparseCore 0:
  12.5 58.4 all-reduce.1
Sparse Core Ops, SparseCore 1:
  13.3 24.8 reduce-scatter.1
where the time goes:
time: 83.7 us; the launch traced here: 83.5 us
  blocking collectives  32.9 us (39%)
  waiting for transfers between devices  24.9 us (30%)
  between operations  15.5 us (19%)
  other arithmetic  6.82 us (8%)
  matrix products  2.62 us (3%)
    psum x1, waiting for transfers between devices, per_device(): delta = lax.psum(drift, 'rep') / replica_count  24.9 us
    all_gather x1, blocking collectives, per_device(): lax.all_gather(weights, 'fsdp', axis=0, tiled=True)  18.9 us
    all_gather x1, blocking collectives, per_device(): moment_all = lax.all_gather(momentum, 'rep', axis=2, tiled=True)  14 us
    add x1, other arithmetic, per_device(): moment_new = outer_beta * moment_all + delta  2.73 us
    sub x1, other arithmetic, per_device(): drift = base - local[0]  2.47 us
  transfers between devices with their start and end apart: 2, of which 1 were waited for; matrix products, arithmetic and copies ran while one was open for 7% of the time, Pallas kernels for 0%

commit v1 on v0

v1 whole, which is shorter than its diff:
```python
import jax
import jax.numpy as jnp
from jax import lax
from jax.sharding import PartitionSpec as P

outer_beta = 0.9
outer_rate = 0.7
mix_keep = 0.5


def send(value, axis, target):
    return lax.ppermute(value, axis, [(i, target(i)) for i in range(lax.axis_size(axis))])


def partner(i, k, n):
    return i ^ k if n & (n - 1) == 0 else (i + k) % n


def by_partner(blocks, index, received):
    n = len(blocks)
    if n & (n - 1):
        stack = jnp.stack(blocks)
        shift = [jnp.mod(index - k if received else index + k, n) for k in range(n)]
        return [lax.dynamic_index_in_dim(stack, s, 0, keepdims=False) for s in shift]
    bit = 1
    while bit < n:
        flip = (index & bit) != 0
        blocks = [jnp.where(flip, blocks[k ^ bit], blocks[k]) for k in range(n)]
        bit *= 2
    return blocks


def by_device(blocks, index):
    n = len(blocks)
    if n & (n - 1):
        stack = jnp.stack(blocks)
        return [lax.dynamic_index_in_dim(stack, jnp.mod(index - j, n), 0, keepdims=False) for j in range(n)]
    return by_partner(blocks, index, True)


def per_device(base, local, momentum, hidden, out_grad):
    n_rep, n_f = lax.axis_size("rep"), lax.axis_size("fsdp")
    f, r = lax.axis_index("fsdp"), lax.axis_index("rep")
    mine, grads = local[0], out_grad[0]
    rows = mine.shape[1]
    weights = lax.optimization_barrier(mine[2].astype(jnp.bfloat16))
    wk = [weights] + [send(weights, "fsdp", lambda i: partner(i, k, n_f)) for k in range(1, n_f)]
    a = (1 + outer_beta) / n_rep
    b = outer_beta * outer_beta
    width = momentum.shape[2]
    half = base.shape[2] // 2
    core = r & 1
    term = (base - mine) * a
    own = lax.dynamic_slice_in_dim(term, r * width, width, 2) + b * momentum
    term = lax.dynamic_update_slice_in_dim(term, own, r * width, 2)
    lo, hi = term[:, :, :half], term[:, :, half:]
    total = jnp.where(core == 0, lo, hi)
    give = jnp.where(core == 0, hi, lo).astype(jnp.bfloat16)
    total = total + send(give, "rep", lambda i: i ^ 1).astype(jnp.float32)
    bits = [1 << k for k in range(1, n_rep.bit_length() - 1)]
    for s in range(len(bits)):
        even, odd = bits[s], bits[(s + 1) % len(bits)]
        got = send(total.astype(jnp.bfloat16), "rep", lambda i: i ^ (odd if i & 1 else even))
        total = total + got.astype(jnp.float32)
    got = send(total.astype(jnp.bfloat16), "rep", lambda i: i ^ 1)
    other = got.astype(jnp.float32)
    step = jnp.concatenate([jnp.where(core == 0, total, other), jnp.where(core == 0, other, total)], axis=2)
    mixed = (mix_keep * mine + (1 - mix_keep) * (base - outer_rate * step))[None]
    own_step = lax.dynamic_slice_in_dim(step, r * width, width, 2)
    momentum_out = outer_beta * momentum + (own_step - b * momentum) / (1 + outer_beta)
    hk = hidden[0].reshape(hidden.shape[1], n_f, rows)
    hk = by_partner([hk[:, k] for k in range(n_f)], f, False)
    part = []
    for k in range(n_f):
        part.append(lax.dot_general(hk[k], grads, (((0,), (0,)), ((), ())),
                                    preferred_element_type=jnp.float32).astype(jnp.bfloat16))
    part[0] = lax.optimization_barrier(part[0])
    got = [send(part[k], "fsdp", lambda i: partner(i, k, n_f)) for k in range(1, n_f)]
    weight_grad = part[0][None].astype(jnp.float32)
    for g in got:
        weight_grad = weight_grad + g[None].astype(jnp.float32)
    input_grad = lax.dot_general(grads, jnp.concatenate(wk, axis=0), (((1,), (1,)), ((), ())),
                                 preferred_element_type=jnp.float32).astype(jnp.bfloat16)
    input_grad = by_device([input_grad[:, k * rows:(k + 1) * rows] for k in range(n_f)], f)
    input_grad = jnp.concatenate(input_grad, axis=1)[None]
    return mixed, momentum_out, input_grad, weight_grad


def solution(mesh):
    return jax.shard_map(
        per_device,
        mesh=mesh,
        in_specs=(P(None, "fsdp", None), P("rep", None, "fsdp", None), P(None, "fsdp", "rep"),
                  P("rep", "fsdp", None), P("rep", "fsdp", None)),
        out_specs=(P("rep", None, "fsdp", None), P(None, "fsdp", "rep"), P("rep", "fsdp", None), P("rep", "fsdp", None)),
        check_vma=False,
    )
```

time: 83.7 us -> 41.2 us (0.49)
  blocking collectives: 32.9 us -> 0 us
  starting transfers between devices: 0.08 us -> 15.3 us
  between operations: 15.5 us -> 0.79 us
  waiting for transfers between devices: 24.9 us -> 15.6 us
  other arithmetic: 6.82 us -> 4.84 us
    all_gather x2 -> x0, blocking collectives: 32.9 us -> none  [the longest x1 18.9 us: per_device(): lax.all_gather(weights, 'fsdp', axis=0, tiled=True)]
    psum x1 -> x0, waiting for transfers between devices: 24.9 us -> none  [per_device(): delta = lax.psum(drift, 'rep') / replica_count]
    ppermute x0 -> x10, waiting for transfers between devices: none -> 15.6 us  [send(): lax.ppermute(value, axis, [(i, target(i)) for i in range(lax.axis_size(ax...]
    ppermute x0 -> x10, starting transfers between devices: none -> 15.3 us  [send(): lax.ppermute(value, axis, [(i, target(i)) for i in range(lax.axis_size(ax...]
    sub x1 -> x0, other arithmetic: 2.47 us -> none  [per_device(): drift = base - local[0]]
    mul x0 -> x1, other arithmetic: none -> 1.46 us  [per_device(): term = (base - mine) * a]
    add x1 -> x2, other arithmetic: 2.73 us -> 1.45 us  [the longest x1 0.77 us: per_device(): weight_grad = weight_grad + g[None].astype(jnp.float32)]
    convert_element_type x0 -> x1, local copies, waits for them, and re-layouts: none -> 1.14 us  [per_device(): weights = lax.optimization_barrier(mine[2].astype(jnp.bfloat16))]
  transfers between devices with their start and end apart: 2 -> 10, of which waited for: 1 -> 5; matrix products, arithmetic and copies ran while one was open for 7% -> 15% of each run, Pallas kernels for 0% -> 0%
where the time goes in v1:
time: 41.2 us; the launch traced here: 41 us
  waiting for transfers between devices  15.6 us (38%)
  starting transfers between devices  15.3 us (37%)
  other arithmetic  4.84 us (12%)
  matrix products  3.28 us (8%)
  local copies, waits for them, and re-layouts  1.18 us (3%)
  between operations  0.79 us (2%)
    ppermute x10, waiting for transfers between devices, send(): lax.ppermute(value, axis, [(i, target(i)) for i in range(lax.axis_size(ax...  15.6 us
    ppermute x10, starting transfers between devices, send(): lax.ppermute(value, axis, [(i, target(i)) for i in range(lax.axis_size(ax...  15.3 us
    dot_general x1, matrix products, per_device(): lax.dot_general(grads, jnp.concatenate(wk, axis=0), (((1,), (1,)), ((), (...  1.76 us
    dot_general x4, matrix products, per_device(): lax.dot_general(hk[k], grads, (((0,), (0,)), ((), ())), preferred_element...  1.52 us
    mul x1, other arithmetic, per_device(): term = (base - mine) * a  1.46 us
    convert_element_type x1, local copies, waits for them, and re-layouts, per_device(): weights = lax.optimization_barrier(mine[2].astype(jnp.bfloat16))  1.14 us
    broadcast_in_dim x1, other arithmetic, per_device(): (mix_keep * mine + (1 - mix_keep) * (base - outer_rate * step))[None]  1.01 us
  transfers between devices with their start and end apart: 10, of which 5 were waited for; matrix products, arithmetic and copies ran while one was open for 15% of the time, Pallas kernels for 0%

profile of v1, /device:TPU:0, one launch (start us, length us, event | category | flops | bytes accessed | tf_op | source)
XLA Modules:
  0.0 41.0 jit_solution(15687465386097869819)
XLA Ops:
  0.6 0.0 copy-start
  0.6 0.0 copy-start.3
  0.7 0.0 copy-start.4
  0.7 1.1 %fusion.26 = bf16[8,8192]{1,0:T(8,128)(2,1)S(1)} fusion(f32[1,3,8,8192]{3,2,1,0:T(8,128)} %param.6), kind=kLoop, calls=%fused_computation.38 | loop fusion | bytes 262144 | tf_op jit(solution)/shard_map/convert_element_type | solution.py:46
  1.8 3.1 %collective-permute-start.4 = (bf16[8,8192]{1,0:T(8,128)(2,1)S(1)}, bf16[8,8192]{1,0:T(8,128)(2,1)}, u32[]{:S(2)}, u32[]{:S(2)}) collective-permute-start(bf16[8,8192]{1,0:T(8,128)(2,1)S(1)} %fusion.26), channel_id=1, source_target_pairs={{0,1},{1,0},{2,3},{3,2},{4,5},{5,4},{6,7},{7,6},{8,9},{9,8},{10,11... | collective-permute-start | bytes 393224 | tf_op jit(solution)/shard_map/ppermute | solution.py:12
  4.9 2.6 %collective-permute-start.5 = (bf16[8,8192]{1,0:T(8,128)(2,1)S(1)}, bf16[8,8192]{1,0:T(8,128)(2,1)}, u32[]{:S(2)}, u32[]{:S(2)}) collective-permute-start(bf16[8,8192]{1,0:T(8,128)(2,1)S(1)} %fusion.26), channel_id=1, source_target_pairs={{0,2},{1,3},{2,0},{3,1},{4,6},{5,7},{6,4},{7,5},{8,10},{9,11},{10,... | collective-permute-start | bytes 393224 | tf_op jit(solution)/shard_map/ppermute | solution.py:12
  7.5 1.5 %fusion.17 = f32[3,8,8192]{2,1,0:T(8,128)S(1)} fusion(f32[3,8,8192]{2,1,0:T(8,128)} %param.5, f32[1,3,8,8192]{3,2,1,0:T(8,128)} %param.6), kind=kLoop, calls=%fused_computation.21 | loop fusion | flops 393216 | bytes 2359296 | tf_op jit(solution)/shard_map/mul | solution.py:53
  9.0 0.0 copy-done.3
  9.1 0.1 collective-permute-start
  9.2 0.0 copy-done
  9.2 0.0 copy-done.4
  9.2 0.4 convolution_convert_fusion.2
  9.6 0.5 %collective-permute-start.7 = (bf16[8,8192]{1,0:T(8,128)(2,1)S(1)}, bf16[8,8192]{1,0:T(8,128)(2,1)S(1)}, u32[]{:S(2)}, u32[]{:S(2)}) collective-permute-start(bf16[8,8192]{1,0:T(8,128)(2,1)S(1)} %convolution_convert_fusion.2), channel_id=1, source_target_pairs={{0,1},{1,0},{2,3},{3,2},{4,5},{5,4},{6,7},{7,6},{8,9},{9,8},{10,11... | collective-permute-start | bytes 393224 | tf_op jit(solution)/shard_map/ppermute | solution.py:12
  10.0 0.4 convolution_convert_fusion.1
  10.4 0.1 collective-permute-start.8
  10.5 0.4 convolution_convert_fusion.3
  10.9 0.4 convolution_convert_fusion
  11.2 0.0 collective-permute-done
  11.3 4.0 %collective-permute-start.9 = (bf16[8,8192]{1,0:T(8,128)(2,1)S(1)}, bf16[8,8192]{1,0:T(8,128)(2,1)S(1)}, u32[]{:S(2)}, u32[]{:S(2)}) collective-permute-start(bf16[8,8192]{1,0:T(8,128)(2,1)S(1)} %convolution_convert_fusion), channel_id=1, source_target_pairs={{0,3},{1,2},{2,1},{3,0},{4,7},{5,6},{6,5},{7,4},{8,11},{9,10},{10,... | collective-permute-start | bytes 393224 | tf_op jit(solution)/shard_map/ppermute | solution.py:12
  15.2 0.1 fusion.45
  15.3 2.3 %collective-permute-done.7 = bf16[8,8192]{1,0:T(8,128)(2,1)S(1)} collective-permute-done((bf16[8,8192]{1,0:T(8,128)(2,1)S(1)}, bf16[8,8192]{1,0:T(8,128)(2,1)S(1)}, u32[]{:S(2)}, u32[]{:S(2)}) %collective-permute-start.7) | collective-permute-done | bytes 131104 | tf_op jit(solution)/shard_map/ppermute | solution.py:12
  17.6 1.9 %collective-permute-start.6 = (bf16[8,8192]{1,0:T(8,128)(2,1)S(1)}, bf16[8,8192]{1,0:T(8,128)(2,1)S(1)}, u32[]{:S(2)}, u32[]{:S(2)}) collective-permute-start(bf16[8,8192]{1,0:T(8,128)(2,1)S(1)} %fusion.26), channel_id=1, source_target_pairs={{0,3},{1,2},{2,1},{3,0},{4,7},{5,6},{6,5},{7,4},{8,11},{9,10},{10,... | collective-permute-start | bytes 393224 | tf_op jit(solution)/shard_map/ppermute | solution.py:12
  19.5 6.7 %collective-permute-done.8 = bf16[8,8192]{1,0:T(8,128)(2,1)S(1)} collective-permute-done((bf16[8,8192]{1,0:T(8,128)(2,1)S(1)}, bf16[8,8192]{1,0:T(8,128)(2,1)S(1)}, u32[]{:S(2)}, u32[]{:S(2)}) %collective-permute-start.8) | collective-permute-done | bytes 131104 | tf_op jit(solution)/shard_map/ppermute | solution.py:12
  26.2 1.5 %collective-permute-start.1 = (bf16[3,8,4096]{2,1,0:T(8,128)(2,1)S(1)}, bf16[3,8,4096]{2,1,0:T(8,128)(2,1)S(1)}, u32[]{:S(2)}, u32[]{:S(2)}) collective-permute-start(bf16[3,8,4096]{2,1,0:T(8,128)(2,1)S(1)} %get-tuple-element.4), channel_id=1, source_target_pairs={{0,8},{4,20},{8,0},{12,28},{16,24},{20,4},{24,16},{28,12},{1,9},{5... | collective-permute-start | bytes 589832 | tf_op jit(solution)/shard_map/ppermute | solution.py:12
  27.7 0.0 collective-permute-done.9
  27.7 0.8 %add_bitcast_fusion = f32[1,8,8192]{2,1,0:T(8,128)} fusion(bf16[8,8192]{1,0:T(8,128)(2,1)S(1)} %collective-permute-done.9, bf16[8,8192]{1,0:T(8,128)(2,1)S(1)} %collective-permute-done.8, bf16[8,8192]{1,0:T(8,128)(2,1)S(1)} %collective-permute-done.7, bf16[8,8192]{1,0:T(8,128)(2,1)S(1)} %convolution_convert_fusion.3), kind=kLoop, calls=%fused_computation.37 | loop fusion | flops 458752 | bytes 786432 | tf_op jit(solution)/shard_map/add | solution.py:81
  28.4 3.4 %collective-permute-done.1 = bf16[3,8,4096]{2,1,0:T(8,128)(2,1)S(1)} collective-permute-done((bf16[3,8,4096]{2,1,0:T(8,128)(2,1)S(1)}, bf16[3,8,4096]{2,1,0:T(8,128)(2,1)S(1)}, u32[]{:S(2)}, u32[]{:S(2)}) %collective-permute-start.1) | collective-permute-done | bytes 196640 | tf_op jit(solution)/shard_map/ppermute | solution.py:12
  31.9 1.6 %collective-permute-start.2 = (bf16[3,8,4096]{2,1,0:T(8,128)(2,1)S(1)}, bf16[3,8,4096]{2,1,0:T(8,128)(2,1)S(1)}, u32[]{:S(2)}, u32[]{:S(2)}) collective-permute-start(bf16[3,8,4096]{2,1,0:T(8,128)(2,1)S(1)} %fusion.25), channel_id=1, source_target_pairs={{0,16},{4,12},{8,24},{12,4},{16,0},{20,28},{24,8},{28,20},{1,17},{... | collective-permute-start | bytes 589832 | tf_op jit(solution)/shard_map/ppermute | solution.py:12
  33.5 0.0 collective-permute-done.4
  33.5 0.0 collective-permute-done.5
  33.5 0.0 collective-permute-done.6
  33.5 1.8 %fusion.9 = bf16[128,32]{0,1:T(8,128)(2,1)S(1)} fusion(bf16[1,128,8192]{2,1,0:T(8,128)(2,1)S(1)} %copy-done, bf16[8,8192]{1,0:T(8,128)(2,1)S(1)} %collective-permute-done.6, bf16[8,8192]{1,0:T(8,128)(2,1)} %collective-permute-done.5, bf16[8,8192]{1,0:T(8,128)(2,1)} %collective-permute-done.4, bf16[8,8192]{1,0:T(8,128)(2,1)S(1)} %fusion.26), kind=kOutput, calls=%fused_computation.11 | convolution fusion | flops 69210112 | bytes 2629632 | tf_op jit(solution)/shard_map/dot_general | solution.py:82
  35.2 0.0 copy-start.1
  35.3 0.0 copy-start.2
  35.3 2.3 %collective-permute-done.2 = bf16[3,8,4096]{2,1,0:T(8,128)(2,1)S(1)} collective-permute-done((bf16[3,8,4096]{2,1,0:T(8,128)(2,1)S(1)}, bf16[3,8,4096]{2,1,0:T(8,128)(2,1)S(1)}, u32[]{:S(2)}, u32[]{:S(2)}) %collective-permute-start.2) | collective-permute-done | bytes 196640 | tf_op jit(solution)/shard_map/ppermute | solution.py:12
  37.6 0.1 fusion.44
  37.7 0.1 collective-permute-start.3
  37.8 0.6 %maximum_bitcast_fusion = bf16[1,128,32]{1,2,0:T(8,128)(2,1)} fusion(bf16[128,8]{0,1:T(8,128)(2,1)S(1)} %get-tuple-element.11, bf16[128,8]{0,1:T(8,128)(2,1)S(1)} %get-tuple-element.10, bf16[128,8]{0,1:T(8,128)(2,1)S(1)} %get-tuple-element.9, bf16[128,8]{0,1:T(8,128)(2,1)S(1)} %get-tuple-element.8), kind=kLoop, calls=%fused_computation.44 | loop fusion | flops 32768 | bytes 16384 | tf_op jit(solution)/shard_map/broadcast_in_dim | solution.py:85
  38.4 0.8 %collective-permute-done.3 = bf16[3,8,4096]{2,1,0:T(8,128)(2,1)S(1)} collective-permute-done((bf16[3,8,4096]{2,1,0:T(8,128)(2,1)S(1)}, bf16[3,8,4096]{2,1,0:T(8,128)(2,1)S(1)}, u32[]{:S(2)}, u32[]{:S(2)}) %collective-permute-start.3) | collective-permute-done | bytes 196640 | tf_op jit(solution)/shard_map/ppermute | solution.py:12
  39.2 0.1 convert_select_fusion.1
  39.3 0.7 %fusion.30 = f32[3,8,1024]{2,1,0:T(8,128)} fusion(s32[]{:T(128)S(6)} %select_n.120, f32[3,8,4096]{2,1,0:T(8,128)S(1)} %get-tuple-element.6, f32[3,8,4096]{2,1,0:T(8,128)S(1)} %get-tuple-element.7, f32[3,8,1024]{2,1,0:T(8,128)S(1)} %copy-done.3), kind=kLoop, calls=%fused_computation.42 | loop fusion | flops 147456 | bytes 983044 | tf_op jit(solution)/shard_map/add | solution.py:70
  40.0 0.0 copy-done.1
  40.0 0.0 copy-done.2
  40.0 1.0 %fusion.16 = f32[1,3,8,8192]{3,2,1,0:T(8,128)} fusion(f32[3,8,8192]{2,1,0:T(8,128)S(1)} %copy-done.2, f32[3,8,4096]{2,1,0:T(8,128)S(1)} %get-tuple-element.7, f32[3,8,4096]{2,1,0:T(8,128)S(1)} %get-tuple-element.6, f32[1,3,8,8192]{3,2,1,0:T(8,128)S(1)} %copy-done.1), kind=kLoop, calls=%fused_computation.19 | loop fusion | flops 983040 | bytes 3145728 | tf_op jit(solution)/shard_map/broadcast_in_dim | solution.py:68
  (4 shorter events, 0.1 us)
Async XLA Ops:
  0.6 8.5 %copy-start = (bf16[1,128,8192]{2,1,0:T(8,128)(2,1)S(1)}, bf16[1,128,8192]{2,1,0:T(8,128)(2,1)}, u32[]{:S(2)}) copy-start(bf16[1,128,8192]{2,1,0:T(8,128)(2,1)} %param.9) | copy-start | bytes 6291460
  0.6 8.3 %copy-start.3 = (f32[3,8,1024]{2,1,0:T(8,128)S(1)}, f32[3,8,1024]{2,1,0:T(8,128)}, u32[]{:S(2)}) copy-start(f32[3,8,1024]{2,1,0:T(8,128)} %param.7) | copy-start | bytes 294916
  0.7 8.5 %copy-start.4 = (bf16[1,128,32]{1,2,0:T(8,128)(2,1)S(1)}, bf16[1,128,32]{1,2,0:T(8,128)(2,1)}, u32[]{:S(2)}) copy-start(bf16[1,128,32]{1,2,0:T(8,128)(2,1)} %param.8) | copy-start | bytes 24580
  1.8 31.7 %collective-permute-start.4 = (bf16[8,8192]{1,0:T(8,128)(2,1)S(1)}, bf16[8,8192]{1,0:T(8,128)(2,1)}, u32[]{:S(2)}, u32[]{:S(2)}) collective-permute-start(bf16[8,8192]{1,0:T(8,128)(2,1)S(1)} %fusion.26), channel_id=1, source_target_pairs={{0,1},{1,0},{2,3},{3,2},{4,5},{5,4},{6,7},{7,6},{8,9},{9,8},{10,11... | collective-permute-start | bytes 393224 | tf_op jit(solution)/shard_map/ppermute | solution.py:12
  4.9 28.5 %collective-permute-start.5 = (bf16[8,8192]{1,0:T(8,128)(2,1)S(1)}, bf16[8,8192]{1,0:T(8,128)(2,1)}, u32[]{:S(2)}, u32[]{:S(2)}) collective-permute-start(bf16[8,8192]{1,0:T(8,128)(2,1)S(1)} %fusion.26), channel_id=1, source_target_pairs={{0,2},{1,3},{2,0},{3,1},{4,6},{5,7},{6,4},{7,5},{8,10},{9,11},{10,... | collective-permute-start | bytes 393224 | tf_op jit(solution)/shard_map/ppermute | solution.py:12
  9.1 2.2 %collective-permute-start = (bf16[3,8,4096]{2,1,0:T(8,128)(2,1)S(1)}, bf16[3,8,4096]{2,1,0:T(8,128)(2,1)S(1)}, u32[]{:S(2)}, u32[]{:S(2)}) collective-permute-start(bf16[3,8,4096]{2,1,0:T(8,128)(2,1)S(1)} %select_convert_fusion), channel_id=1, source_target_pairs={{0,4},{4,0},{8,12},{12,8},{16,20},{20,16},{24,28},{28,24},{1,5},{5... | collective-permute-start | bytes 589832 | tf_op jit(solution)/shard_map/ppermute | solution.py:12
  9.6 8.1 %collective-permute-start.7 = (bf16[8,8192]{1,0:T(8,128)(2,1)S(1)}, bf16[8,8192]{1,0:T(8,128)(2,1)S(1)}, u32[]{:S(2)}, u32[]{:S(2)}) collective-permute-start(bf16[8,8192]{1,0:T(8,128)(2,1)S(1)} %convolution_convert_fusion.2), channel_id=1, source_target_pairs={{0,1},{1,0},{2,3},{3,2},{4,5},{5,4},{6,7},{7,6},{8,9},{9,8},{10,11... | collective-permute-start | bytes 393224 | tf_op jit(solution)/shard_map/ppermute | solution.py:12
  10.4 15.7 %collective-permute-start.8 = (bf16[8,8192]{1,0:T(8,128)(2,1)S(1)}, bf16[8,8192]{1,0:T(8,128)(2,1)S(1)}, u32[]{:S(2)}, u32[]{:S(2)}) collective-permute-start(bf16[8,8192]{1,0:T(8,128)(2,1)S(1)} %convolution_convert_fusion.1), channel_id=1, source_target_pairs={{0,2},{1,3},{2,0},{3,1},{4,6},{5,7},{6,4},{7,5},{8,10},{9,11},{10,... | collective-permute-start | bytes 393224 | tf_op jit(solution)/shard_map/ppermute | solution.py:12
  11.3 16.4 %collective-permute-start.9 = (bf16[8,8192]{1,0:T(8,128)(2,1)S(1)}, bf16[8,8192]{1,0:T(8,128)(2,1)S(1)}, u32[]{:S(2)}, u32[]{:S(2)}) collective-permute-start(bf16[8,8192]{1,0:T(8,128)(2,1)S(1)} %convolution_convert_fusion), channel_id=1, source_target_pairs={{0,3},{1,2},{2,1},{3,0},{4,7},{5,6},{6,5},{7,4},{8,11},{9,10},{10,... | collective-permute-start | bytes 393224 | tf_op jit(solution)/shard_map/ppermute | solution.py:12
  17.6 15.8 %collective-permute-start.6 = (bf16[8,8192]{1,0:T(8,128)(2,1)S(1)}, bf16[8,8192]{1,0:T(8,128)(2,1)S(1)}, u32[]{:S(2)}, u32[]{:S(2)}) collective-permute-start(bf16[8,8192]{1,0:T(8,128)(2,1)S(1)} %fusion.26), channel_id=1, source_target_pairs={{0,3},{1,2},{2,1},{3,0},{4,7},{5,6},{6,5},{7,4},{8,11},{9,10},{10,... | collective-permute-start | bytes 393224 | tf_op jit(solution)/shard_map/ppermute | solution.py:12
  26.2 5.7 %collective-permute-start.1 = (bf16[3,8,4096]{2,1,0:T(8,128)(2,1)S(1)}, bf16[3,8,4096]{2,1,0:T(8,128)(2,1)S(1)}, u32[]{:S(2)}, u32[]{:S(2)}) collective-permute-start(bf16[3,8,4096]{2,1,0:T(8,128)(2,1)S(1)} %get-tuple-element.4), channel_id=1, source_target_pairs={{0,8},{4,20},{8,0},{12,28},{16,24},{20,4},{24,16},{28,12},{1,9},{5... | collective-permute-start | bytes 589832 | tf_op jit(solution)/shard_map/ppermute | solution.py:12
  31.9 5.7 %collective-permute-start.2 = (bf16[3,8,4096]{2,1,0:T(8,128)(2,1)S(1)}, bf16[3,8,4096]{2,1,0:T(8,128)(2,1)S(1)}, u32[]{:S(2)}, u32[]{:S(2)}) collective-permute-start(bf16[3,8,4096]{2,1,0:T(8,128)(2,1)S(1)} %fusion.25), channel_id=1, source_target_pairs={{0,16},{4,12},{8,24},{12,4},{16,0},{20,28},{24,8},{28,20},{1,17},{... | collective-permute-start | bytes 589832 | tf_op jit(solution)/shard_map/ppermute | solution.py:12
  35.2 4.7 %copy-start.1 = (f32[1,3,8,8192]{3,2,1,0:T(8,128)S(1)}, f32[1,3,8,8192]{3,2,1,0:T(8,128)}, u32[]{:S(2)}) copy-start(f32[1,3,8,8192]{3,2,1,0:T(8,128)} %param.6) | copy-start | bytes 2359300
  35.3 4.7 %copy-start.2 = (f32[3,8,8192]{2,1,0:T(8,128)S(1)}, f32[3,8,8192]{2,1,0:T(8,128)}, u32[]{:S(2)}) copy-start(f32[3,8,8192]{2,1,0:T(8,128)} %param.5) | copy-start | bytes 2359300
  37.7 1.5 %collective-permute-start.3 = (bf16[3,8,4096]{2,1,0:T(8,128)(2,1)S(1)}, bf16[3,8,4096]{2,1,0:T(8,128)(2,1)S(1)}, u32[]{:S(2)}, u32[]{:S(2)}) collective-permute-start(bf16[3,8,4096]{2,1,0:T(8,128)(2,1)S(1)} %fusion.44), channel_id=1, source_target_pairs={{0,4},{4,0},{8,12},{12,8},{16,20},{20,16},{24,28},{28,24},{1,5},{5... | collective-permute-start | bytes 589832 | tf_op jit(solution)/shard_map/ppermute | solution.py:12
